TPU v7x, 256 devices: a whole 4x4x8 slice. The times are simulated.
256 devices in a mesh: lat: 16 (over y_lo, x, core), lon: 16 (over z, y_hi).
Axes of the slice: x: 4, y: 4 (y_hi: 2, y_lo: 2; y = y_hi * 2 + y_lo), z: 8, core: 2. Of those that a mesh axis runs over, the one named last changes fastest.
Arguments:
- fields: bfloat16 [512, 512, 256], P('lat', 'lon'), may hold values from -6 to 6
- w_conv1: bfloat16 [3, 3, 256, 256], replicated, may hold values from -0.125 to 0.125
- b_conv1: float32 [256], replicated, may hold values from -3 to 3
- w_conv2: bfloat16 [3, 3, 256, 256], replicated, may hold values from -0.125 to 0.125
- b_conv2: float32 [256], replicated, may hold values from -3 to 3
- w_query: bfloat16 [256, 256], replicated, may hold values from -16 to 16
- w_key: bfloat16 [256, 64], replicated, may hold values from -1 to 1
- w_value: bfloat16 [256, 64], replicated, may hold values from -0.375 to 0.375
- w_out: bfloat16 [256, 256], replicated, may hold values from -0.375 to 0.375
- rotation: int32 [16, 16], replicated, may hold values from 0 to 3
- owner: int32 [16, 16], replicated, may hold values from 0 to 15, as said below
- counts: int32 [512], replicated, may hold values from 4 to 512
Outputs:
- fields_out: bfloat16 [512, 512, 256], P('lat', 'lon')
Inputs may be any that keep to these rules, and one draw needn't show every extreme that they name: Each row of owner holds every number from 0 to 15 exactly once.
All inputs are finite; a program needn't handle non-finite values.
Results may differ from a plain program's by a relative error of at most 0.014.
Values may be sent and summed in bfloat16 or wider, within the bound.
A program may use at most 64 MiB of HBM per device.

v0:
```python
import math
import jax
import jax.numpy as jnp
from jax import lax
from jax.sharding import PartitionSpec as P


def shortened(x):

    def short(part):
        return part.astype(jnp.bfloat16) if part.dtype == jnp.float32 else part

    return jax.tree.map(short, x)


def passed_along(x, axis, by):
    devices = lax.axis_size(axis)
    pairs = [(i, i + by) for i in range(devices) if 0 <= i + by < devices]
    return lax.ppermute(x, axis, pairs)


def turn_block(block, quarter_turns):
    options = [lambda m, k=k: jnp.rot90(m, k, axes=(0, 1)) for k in range(4)]
    return lax.switch(quarter_turns % 4, options, block)


def inverse_owner(owner):
    shards = jnp.arange(owner.shape[1], dtype=jnp.int32)
    matches = owner[:, None, :] == shards[None, :, None]
    return jnp.sum(jnp.where(matches, shards[None, None, :], 0), axis=2)


def live_region(counts, first_row, row_count, first_col, col_count, total_cols):
    padded_counts = jnp.pad(counts, 2)
    row_limits = lax.dynamic_slice_in_dim(padded_counts, first_row + 2, row_count)
    columns = (first_col + jnp.arange(col_count, dtype=jnp.int32)) % total_cols
    return (columns[None, :] < row_limits[:, None]).astype(jnp.float32)


def pick_block(stack, inverse, band_row, segment):
    return lax.dynamic_index_in_dim(stack, inverse[band_row, segment], 0, keepdims=False)


def fetch_halo(part, width, inverse, band_index, segment):
    lat_size = lax.axis_size("lat")
    lon_size = lax.axis_size("lon")
    block_size = part.shape[0]
    chans = part.shape[2]
    from_north = passed_along(shortened(part[-width:]), "lat", 1)
    from_south = passed_along(shortened(part[:width]), "lat", -1)
    west_all, east_all, north_all, south_all = (
        lax.all_gather(shortened(part[:, :width]), "lon", axis=0, tiled=True),
        lax.all_gather(shortened(part[:, -width:]), "lon", axis=0, tiled=True),
        lax.all_gather(shortened(from_north), "lon", axis=0, tiled=True).astype(from_north.dtype),
        lax.all_gather(shortened(from_south), "lon", axis=0, tiled=True).astype(from_south.dtype),
    )
    west_all = west_all.reshape(lon_size, block_size, width, chans)
    east_all = east_all.reshape(lon_size, block_size, width, chans)
    north_all = north_all.reshape(lon_size, width, block_size, chans)
    south_all = south_all.reshape(lon_size, width, block_size, chans)
    west_segment = (segment - 1) % lon_size
    east_segment = (segment + 1) % lon_size
    north_band = jnp.maximum(band_index - 1, 0)
    south_band = jnp.minimum(band_index + 1, lat_size - 1)
    left_cols = pick_block(east_all, inverse, band_index, west_segment)
    right_cols = pick_block(west_all, inverse, band_index, east_segment)
    upper = jnp.concatenate(
        [
            pick_block(north_all, inverse, north_band, west_segment)[:, -width:],
            pick_block(north_all, inverse, north_band, segment),
            pick_block(north_all, inverse, north_band, east_segment)[:, :width],
        ],
        axis=1,
    )
    lower = jnp.concatenate(
        [
            pick_block(south_all, inverse, south_band, west_segment)[:, -width:],
            pick_block(south_all, inverse, south_band, segment),
            pick_block(south_all, inverse, south_band, east_segment)[:, :width],
        ],
        axis=1,
    )
    middle = jnp.concatenate([left_cols, part, right_cols], axis=1)
    return jnp.concatenate([upper, middle, lower], axis=0)


def convolve(padded, weight, bias, out_rows, out_cols):
    chans = padded.shape[2]
    total = jnp.zeros((out_rows * out_cols, chans), jnp.float32) + bias
    for i in range(3):
        for j in range(3):
            window = padded[i : i + out_rows, j : j + out_cols].reshape(out_rows * out_cols, chans)
            total = total + jnp.dot(window, weight[i, j], preferred_element_type=jnp.float32)
    return total.reshape(out_rows, out_cols, chans)


def on_device(
    fields,
    w_conv1,
    b_conv1,
    w_conv2,
    b_conv2,
    w_query,
    w_key,
    w_value,
    w_out,
    rotation,
    owner,
    counts,
):
    block_size = fields.shape[0]
    chans = fields.shape[2]
    head_dim = w_key.shape[1]
    heads = chans // head_dim
    lon_size = lax.axis_size("lon")
    band_index = lax.axis_index("lat")
    shard_index = lax.axis_index("lon")
    quarter = rotation[band_index, shard_index]
    segment = owner[band_index, shard_index]
    owner_row = owner[band_index]
    inverse = inverse_owner(owner)
    upright = turn_block(fields, (4 - quarter) % 4)
    total_cols = block_size * lon_size
    first_row = band_index * block_size
    first_col = segment * block_size
    live_own = live_region(counts, first_row, block_size, first_col, block_size, total_cols)[
        :, :, None
    ]
    padded = fetch_halo(upright, 1, inverse, band_index, segment)
    first = convolve(padded, w_conv1, b_conv1, block_size, block_size)
    act = (jax.nn.silu(first) * live_own).astype(jnp.bfloat16)
    act_padded = fetch_halo(act, 1, inverse, band_index, segment)
    second = convolve(act_padded, w_conv2, b_conv2, block_size, block_size)
    mixed = ((upright.astype(jnp.float32) + second) * live_own).astype(jnp.bfloat16)
    flat = mixed.reshape(block_size * block_size, chans).astype(jnp.float32)
    normed = (flat * lax.rsqrt(jnp.mean(flat * flat, axis=1, keepdims=True) + 1e-06)).astype(
        jnp.bfloat16
    )
    query = jnp.dot(normed, w_query, preferred_element_type=jnp.float32).astype(jnp.bfloat16)
    query = query.reshape(block_size, block_size, chans)
    key_val = jnp.dot(
        normed, jnp.concatenate([w_key, w_value], axis=1), preferred_element_type=jnp.float32
    )
    key_val = key_val.astype(jnp.bfloat16).reshape(block_size, block_size, 2 * head_dim)
    root_dim = math.sqrt(head_dim)
    heads_q = query.reshape(block_size, block_size, heads, head_dim)
    row_limits = lax.dynamic_slice_in_dim(counts, first_row, block_size)
    piece = lax.all_gather(key_val, "lon", axis=1, tiled=True)
    summed = jnp.zeros((block_size, block_size, heads, head_dim), jnp.float32)
    peak = jnp.full((block_size, block_size, heads), -jnp.inf, jnp.float32)
    total = jnp.zeros((block_size, block_size, heads), jnp.float32)
    positions = jnp.arange(piece.shape[1], dtype=jnp.int32)
    true_cols = owner_row[positions // block_size] * block_size + positions % block_size
    live_keys = true_cols[None, :] < row_limits[:, None]
    scores = (
        jnp.einsum(
            "rchd,rkd->rchk", heads_q, piece[:, :, :head_dim], preferred_element_type=jnp.float32
        )
        / root_dim
    )
    scores = jnp.where(live_keys[:, None, None, :], scores, -jnp.inf)
    new_peak = jnp.max(scores, axis=3)
    safe_peak = jnp.where(jnp.isfinite(new_peak), new_peak, 0.0)
    expo = jnp.exp(scores - safe_peak[..., None])
    shrink = jnp.exp(peak - safe_peak)
    total = total * shrink + jnp.sum(expo, axis=3)
    summed = summed * shrink[..., None] + jnp.einsum(
        "rchk,rkd->rchd",
        expo.astype(jnp.bfloat16),
        piece[:, :, head_dim:],
        preferred_element_type=jnp.float32,
    )
    summed, peak, total = (summed, new_peak, total)
    attended = (
        (summed / total[..., None]).astype(jnp.bfloat16).reshape(block_size * block_size, chans)
    )
    update = jnp.dot(attended, w_out, preferred_element_type=jnp.float32).reshape(
        block_size, block_size, chans
    )
    result = (mixed.astype(jnp.float32) + update * live_own).astype(jnp.bfloat16)
    return turn_block(result, quarter)


def solution(mesh):
    in_specs = (P("lat", "lon", None), P(), P(), P(), P(), P(), P(), P(), P(), P(), P(), P())
    out_specs = P("lat", "lon", None)
    return jax.shard_map(
        on_device, mesh=mesh, in_specs=in_specs, out_specs=out_specs, check_vma=False
    )
```

profile of v0, /device:TPU:2, one launch (start us, length us, event | category | flops | bytes accessed | tf_op | source)
XLA Modules:
  0.0 503.1 jit_solution(5571521871443634493)
XLA Ops:
  6.5 1.3 dynamic_slice.73
  8.5 1.1 conditional.2
  10.0 1.9 collective-permute-start.1
  11.9 2.4 collective-permute-start
  22.9 46.0 %all_gather.28 = bf16[512,1,256]{2,0,1:T(8,128)(2,1)S(1)} all-gather(bf16[32,1,256]{2,0,1:T(8,128)(2,1)S(1)} %get-tuple-element.55), channel_id=1, replica_groups=mesh['lat'=16,'lon'=16] {'lon'}, dimensions={0}, use_global_device_ids=true | all-gather | bytes 278528 | tf_op jit(solution)/shard_map/all_gather | solution.py:53
  69.6 36.9 %all_gather.29 = bf16[512,1,256]{2,0,1:T(8,128)(2,1)S(1)} all-gather(bf16[32,1,256]{2,0,1:T(8,128)(2,1)S(1)} %get-tuple-element.56), channel_id=1, replica_groups=mesh['lat'=16,'lon'=16] {'lon'}, dimensions={0}, use_global_device_ids=true | all-gather | bytes 278528 | tf_op jit(solution)/shard_map/all_gather | solution.py:52
  119.1 40.5 %all_gather.27 = bf16[16,32,256]{2,1,0:T(8,128)(2,1)S(1)} all-gather(bf16[1,32,256]{2,1,0:T(8,128)(2,1)S(1)} %collective-permute-done), channel_id=1, replica_groups=mesh['lat'=16,'lon'=16] {'lon'}, dimensions={0}, use_global_device_ids=true | all-gather | bytes 278528 | tf_op jit(solution)/shard_map/all_gather | solution.py:54
  159.7 37.0 %all_gather.30 = bf16[16,32,256]{2,1,0:T(8,128)(2,1)S(1)} all-gather(bf16[1,32,256]{2,1,0:T(8,128)(2,1)S(1)} %collective-permute-done.1), channel_id=1, replica_groups=mesh['lat'=16,'lon'=16] {'lon'}, dimensions={0}, use_global_device_ids=true | all-gather | bytes 278528 | tf_op jit(solution)/shard_map/all_gather | solution.py:55
  201.5 1.9 collective-permute-start.3
  203.5 2.4 collective-permute-start.2
  205.9 40.5 %all_gather.33 = bf16[512,1,256]{2,0,1:T(8,128)(2,1)S(1)} all-gather(bf16[32,1,256]{2,0,1:T(8,128)(2,1)S(1)} %copy.114), channel_id=1, replica_groups=mesh['lat'=16,'lon'=16] {'lon'}, dimensions={0}, use_global_device_ids=true | all-gather | bytes 278528 | tf_op jit(solution)/shard_map/all_gather | solution.py:52
  246.4 37.2 %all_gather.32 = bf16[512,1,256]{2,0,1:T(8,128)(2,1)S(1)} all-gather(bf16[32,1,256]{2,0,1:T(8,128)(2,1)S(1)} %copy.113), channel_id=1, replica_groups=mesh['lat'=16,'lon'=16] {'lon'}, dimensions={0}, use_global_device_ids=true | all-gather | bytes 278528 | tf_op jit(solution)/shard_map/all_gather | solution.py:53
  284.2 40.2 %all_gather.31 = bf16[16,32,256]{2,1,0:T(8,128)(2,1)S(1)} all-gather(bf16[1,32,256]{2,1,0:T(8,128)(2,1)S(1)} %collective-permute-done.2), channel_id=1, replica_groups=mesh['lat'=16,'lon'=16] {'lon'}, dimensions={0}, use_global_device_ids=true | all-gather | bytes 278528 | tf_op jit(solution)/shard_map/all_gather | solution.py:54
  324.4 37.5 %all_gather.34 = bf16[16,32,256]{2,1,0:T(8,128)(2,1)S(1)} all-gather(bf16[1,32,256]{2,1,0:T(8,128)(2,1)S(1)} %collective-permute-done.3), channel_id=1, replica_groups=mesh['lat'=16,'lon'=16] {'lon'}, dimensions={0}, use_global_device_ids=true | all-gather | bytes 278528 | tf_op jit(solution)/shard_map/all_gather | solution.py:55
  372.2 4.4 compare_select_fusion.1
  376.6 5.6 %fusion.63 = s32[512]{0:T(512)S(1)} fusion(pred[512]{0:T(512)(128)(4,1)S(1)} %get-tuple-element.95, pred[512]{0:T(512)(128)(4,1)S(1)} %get-tuple-element.96, pred[512]{0:T(512)(128)(4,1)S(1)} %get-tuple-element.97, pred[512]{0:T(512)(128)(4,1)S(1)} %get-tuple-element.98, pred[512]{0:T(512)(128)(4,1)S(1)} %get-tuple-element.99, ...), kind=kLoop, calls=%fused_computation.145 | loop fusion | flops 8704 | bytes 8740 | tf_op jit(solution)/shard_map/add | solution.py:153
  382.6 1.5 reshape_reshape.3
  384.1 82.8 %all-gather.2.cloned.1.call-done = bf16[32,512,128]{2,0,1:T(8,128)(2,1)} async-done(((bf16[32,32,128]{2,0,1:T(8,128)(2,1)}), bf16[32,512,128]{2,0,1:T(8,128)(2,1)}) %all-gather.2.cloned.1.call-update) | async-done | bytes 4194320 | tf_op jit(solution)/shard_map/all_gather | solution.py:148
  466.9 7.6 %fusion.74 = (bf16[32,512,64]{2,0,1:T(8,128)(2,1)}, bf16[32,512,64]{2,0,1:T(8,128)(2,1)}) fusion(bf16[32,512,128]{2,0,1:T(8,128)(2,1)} %all-gather.2.cloned.1.call-done), kind=kLoop, calls=%fused_computation.158 | loop fusion | bytes 8388608 | tf_op jit(solution)/shard_map/slice | solution.py:157
  474.5 4.5 copy.133
  478.9 5.5 %copy.134 = bf16[32,512,64]{1,2,0:T(8,128)(2,1)} copy(bf16[32,512,64]{2,0,1:T(8,128)(2,1)} %get-tuple-element.28) | data formatting | bytes 4194304
  484.4 2.6 fusion
  487.0 2.4 fusion.1
  489.5 2.9 divide_convert_fusion
  (115 shorter events, 22.5 us)
Async XLA Ops:
  6.5 375.8 %copy-start = (bf16[256,256]{1,0:T(8,128)(2,1)S(1)}, bf16[256,256]{1,0:T(8,128)(2,1)}, u32[]{:S(2)}) copy-start(bf16[256,256]{1,0:T(8,128)(2,1)} %param.25) | copy-start | bytes 393220
  6.5 460.3 %all-gather.2.cloned.1.call-start = ((), (), s32[]{:S(2)}) async-start(), calls=%async_computation | async-start | bytes 4456448 | tf_op jit(solution)/shard_map/all_gather | solution.py:148
  8.5 5.8 %copy-start.9 = (s32[16,16]{1,0:T(8,128)S(1)}, s32[16,16]{1,0:T(8,128)}, u32[]{:S(2)}) copy-start(s32[16,16]{1,0:T(8,128)} %param.30) | copy-start | bytes 3076
  8.5 14.0 %copy-start.10 = (s32[512]{0:T(512)S(1)}, s32[512]{0:T(512)}, u32[]{:S(2)}) copy-start(s32[512]{0:T(512)} %param.31) | copy-start | bytes 6148
  10.0 149.7 %collective-permute-start.1 = (bf16[1,32,256]{2,1,0:T(8,128)(2,1)S(1)}, bf16[1,32,256]{2,1,0:T(8,128)(2,1)S(1)}, u32[]{:S(2)}, u32[]{:S(2)}) collective-permute-start(bf16[1,32,256]{2,1,0:T(8,128)(2,1)S(1)} %get-tuple-element.51), channel_id=1, source_target_pairs={{16,0},{32,16},{48,32},{64,48},{80,64},{96,80},{112,96},{128,112},... | collective-permute-start | bytes 49160 | tf_op jit(solution)/shard_map/ppermute | solution.py:19
  11.9 107.2 %collective-permute-start = (bf16[1,32,256]{2,1,0:T(8,128)(2,1)S(1)}, bf16[1,32,256]{2,1,0:T(8,128)(2,1)S(1)}, u32[]{:S(2)}, u32[]{:S(2)}) collective-permute-start(bf16[1,32,256]{2,1,0:T(8,128)(2,1)S(1)} %get-tuple-element.52), channel_id=1, source_target_pairs={{0,16},{16,32},{32,48},{48,64},{64,80},{80,96},{96,112},{112,128},... | collective-permute-start | bytes 49160 | tf_op jit(solution)/shard_map/ppermute | solution.py:19
  197.2 1.3 copy-start.4
  197.2 1.3 copy-start.11
  201.5 122.9 %collective-permute-start.3 = (bf16[1,32,256]{2,1,0:T(8,128)(2,1)S(1)}, bf16[1,32,256]{2,1,0:T(8,128)(2,1)S(1)}, u32[]{:S(2)}, u32[]{:S(2)}) collective-permute-start(bf16[1,32,256]{2,1,0:T(8,128)(2,1)S(1)} %get-tuple-element.45), channel_id=1, source_target_pairs={{16,0},{32,16},{48,32},{64,48},{80,64},{96,80},{112,96},{128,112},... | collective-permute-start | bytes 49160 | tf_op jit(solution)/shard_map/ppermute | solution.py:19
  203.5 80.7 %collective-permute-start.2 = (bf16[1,32,256]{2,1,0:T(8,128)(2,1)S(1)}, bf16[1,32,256]{2,1,0:T(8,128)(2,1)S(1)}, u32[]{:S(2)}, u32[]{:S(2)}) collective-permute-start(bf16[1,32,256]{2,1,0:T(8,128)(2,1)S(1)} %get-tuple-element.46), channel_id=1, source_target_pairs={{0,16},{16,32},{32,48},{48,64},{64,80},{80,96},{96,112},{112,128},... | collective-permute-start | bytes 49160 | tf_op jit(solution)/shard_map/ppermute | solution.py:19
  362.9 1.3 copy-start.5
  362.9 1.3 copy-start.12
  367.6 0.8 copy-start.7
  367.6 0.8 copy-start.8
  487.0 2.5 copy-start.3
  492.3 1.2 copy-start.6
  494.6 0.8 copy-start.2
  495.4 0.9 copy-start.1
Sparse Core Ops, SparseCore 0:
  369.6 97.2 all-gather.1
where the time goes:
time: 504 us; the launch traced here: 503 us
  blocking collectives  316 us (63%)
  waiting for transfers between devices  82.8 us (16%)
  between operations  35.8 us (7%)
  local copies, waits for them, and re-layouts  32 us (6%)
  other arithmetic  16.2 us (3%)
  matrix products  11.8 us (2%)
  starting transfers between devices  8.66 us (2%)
    all_gather x2, blocking collectives, fetch_halo(): lax.all_gather(shortened(part[:, -width:]), 'lon', axis=0, tiled=True)  83.2 us
    all_gather x1, waiting for transfers between devices, on_device(): piece = lax.all_gather(key_val, 'lon', axis=1, tiled=True)  82.8 us
    all_gather x2, blocking collectives, fetch_halo(): lax.all_gather(shortened(from_north), 'lon', axis=0, tiled=True)  80.8 us
    all_gather x2, blocking collectives, fetch_halo(): lax.all_gather(shortened(part[:, :width]), 'lon', axis=0, tiled=True)  77.4 us
    all_gather x2, blocking collectives, fetch_halo(): lax.all_gather(shortened(from_south), 'lon', axis=0, tiled=True)  74.5 us
    unnamed x28, local copies, waits for them, and re-layouts  13.4 us
  transfers between devices with their start and end apart: 5, of which 1 were waited for; matrix products, arithmetic and copies ran while one was open for 3% of the time, Pallas kernels for 0%

commit v1 on v0

--- a/solution.py
+++ b/solution.py
@@ -145,7 +145,9 @@
     root_dim = math.sqrt(head_dim)
     heads_q = query.reshape(block_size, block_size, heads, head_dim)
     row_limits = lax.dynamic_slice_in_dim(counts, first_row, block_size)
-    piece = lax.all_gather(key_val, "lon", axis=1, tiled=True)
+    piece = jnp.concatenate(
+        lax.all_to_all(jnp.stack([key_val] * lax.axis_size("lon")), "lon", 0, 0), axis=1
+    )
     summed = jnp.zeros((block_size, block_size, heads, head_dim), jnp.float32)
     peak = jnp.full((block_size, block_size, heads), -jnp.inf, jnp.float32)
     total = jnp.zeros((block_size, block_size, heads), jnp.float32)

time: 504 us -> 459 us (0.911)
  waiting for transfers between devices: 82.8 us -> 43.6 us
  between operations: 35.8 us -> 21.9 us
  local copies, waits for them, and re-layouts: 32 us -> 18.7 us
  starting transfers between devices: 8.66 us -> 19.5 us
  blocking collectives: 316 us -> 324 us
    all_gather x1 -> x0, waiting for transfers between devices: 82.8 us -> none  [on_device(): piece = lax.all_gather(key_val, 'lon', axis=1, tiled=True)]
    all_to_all x0 -> x1, waiting for transfers between devices: none -> 43.6 us  [on_device(): lax.all_to_all(jnp.stack([key_val] * lax.axis_size('lon')), 'lon', 0, 0)]
    all_to_all x0 -> x1, starting transfers between devices: none -> 10.8 us  [on_device(): lax.all_to_all(jnp.stack([key_val] * lax.axis_size('lon')), 'lon', 0, 0)]
    unnamed x28 -> x24, local copies, waits for them, and re-layouts: 13.4 us -> 3.53 us
    all_gather x2, blocking collectives: 74.5 us -> 82.6 us  [fetch_halo(): lax.all_gather(shortened(from_south), 'lon', axis=0, tiled=True)]
    slice x1 -> x0, local copies, waits for them, and re-layouts: 7.59 us -> none  [on_device(): piece[:, :, :head_dim]]
where the time goes in v1:
time: 459 us; the launch traced here: 456 us
  blocking collectives  324 us (71%)
  waiting for transfers between devices  43.6 us (9%)
  between operations  21.9 us (5%)
  starting transfers between devices  19.5 us (4%)
  local copies, waits for them, and re-layouts  18.7 us (4%)
  other arithmetic  16 us (3%)
  matrix products  12.4 us (3%)
    all_gather x2, blocking collectives, fetch_halo(): lax.all_gather(shortened(part[:, -width:]), 'lon', axis=0, tiled=True)  83.2 us
    all_gather x2, blocking collectives, fetch_halo(): lax.all_gather(shortened(from_south), 'lon', axis=0, tiled=True)  82.6 us
    all_gather x2, blocking collectives, fetch_halo(): lax.all_gather(shortened(from_north), 'lon', axis=0, tiled=True)  80.8 us
    all_gather x2, blocking collectives, fetch_halo(): lax.all_gather(shortened(part[:, :width]), 'lon', axis=0, tiled=True)  77.4 us
    all_to_all x1, waiting for transfers between devices, on_device(): lax.all_to_all(jnp.stack([key_val] * lax.axis_size('lon')), 'lon', 0, 0)  43.6 us
    all_to_all x1, starting transfers between devices, on_device(): lax.all_to_all(jnp.stack([key_val] * lax.axis_size('lon')), 'lon', 0, 0)  10.8 us
  transfers between devices with their start and end apart: 5, of which 1 were waited for; matrix products, arithmetic and copies ran while one was open for 3% of the time, Pallas kernels for 0%

profile of v1, /device:TPU:2, one launch (start us, length us, event | category | flops | bytes accessed | tf_op | source)
XLA Modules:
  0.0 456.2 jit_solution(6393467648494600784)
XLA Ops:
  0.0 1.3 dynamic_slice.73
  2.0 1.1 conditional.2
  2.0 1.1 rev.22
  3.4 1.9 collective-permute-start.1
  5.4 2.4 collective-permute-start
  16.1 46.0 %all_gather.25 = bf16[512,1,256]{2,0,1:T(8,128)(2,1)S(1)} all-gather(bf16[32,1,256]{2,0,1:T(8,128)(2,1)S(1)} %get-tuple-element.53), channel_id=1, replica_groups=mesh['lat'=16,'lon'=16] {'lon'}, dimensions={0}, use_global_device_ids=true | all-gather | bytes 278528 | tf_op jit(solution)/shard_map/all_gather | solution.py:53
  62.7 36.9 %all_gather.26 = bf16[512,1,256]{2,0,1:T(8,128)(2,1)S(1)} all-gather(bf16[32,1,256]{2,0,1:T(8,128)(2,1)S(1)} %get-tuple-element.54), channel_id=1, replica_groups=mesh['lat'=16,'lon'=16] {'lon'}, dimensions={0}, use_global_device_ids=true | all-gather | bytes 278528 | tf_op jit(solution)/shard_map/all_gather | solution.py:52
  112.0 40.5 %all_gather.24 = bf16[16,32,256]{2,1,0:T(8,128)(2,1)S(1)} all-gather(bf16[1,32,256]{2,1,0:T(8,128)(2,1)S(1)} %collective-permute-done), channel_id=1, replica_groups=mesh['lat'=16,'lon'=16] {'lon'}, dimensions={0}, use_global_device_ids=true | all-gather | bytes 278528 | tf_op jit(solution)/shard_map/all_gather | solution.py:54
  152.6 37.0 %all_gather.27 = bf16[16,32,256]{2,1,0:T(8,128)(2,1)S(1)} all-gather(bf16[1,32,256]{2,1,0:T(8,128)(2,1)S(1)} %collective-permute-done.1), channel_id=1, replica_groups=mesh['lat'=16,'lon'=16] {'lon'}, dimensions={0}, use_global_device_ids=true | all-gather | bytes 278528 | tf_op jit(solution)/shard_map/all_gather | solution.py:55
  194.5 1.9 collective-permute-start.3
  196.4 2.4 collective-permute-start.2
  198.8 40.5 %all_gather.30 = bf16[512,1,256]{2,0,1:T(8,128)(2,1)S(1)} all-gather(bf16[32,1,256]{2,0,1:T(8,128)(2,1)S(1)} %copy.116), channel_id=1, replica_groups=mesh['lat'=16,'lon'=16] {'lon'}, dimensions={0}, use_global_device_ids=true | all-gather | bytes 278528 | tf_op jit(solution)/shard_map/all_gather | solution.py:52
  239.4 37.2 %all_gather.29 = bf16[512,1,256]{2,0,1:T(8,128)(2,1)S(1)} all-gather(bf16[32,1,256]{2,0,1:T(8,128)(2,1)S(1)} %copy.115), channel_id=1, replica_groups=mesh['lat'=16,'lon'=16] {'lon'}, dimensions={0}, use_global_device_ids=true | all-gather | bytes 278528 | tf_op jit(solution)/shard_map/all_gather | solution.py:53
  277.1 40.2 %all_gather.28 = bf16[16,32,256]{2,1,0:T(8,128)(2,1)S(1)} all-gather(bf16[1,32,256]{2,1,0:T(8,128)(2,1)S(1)} %collective-permute-done.2), channel_id=1, replica_groups=mesh['lat'=16,'lon'=16] {'lon'}, dimensions={0}, use_global_device_ids=true | all-gather | bytes 278528 | tf_op jit(solution)/shard_map/all_gather | solution.py:54
  317.4 45.6 %all_gather.31 = bf16[16,32,256]{2,1,0:T(8,128)(2,1)S(1)} all-gather(bf16[1,32,256]{2,1,0:T(8,128)(2,1)S(1)} %collective-permute-done.3), channel_id=1, replica_groups=mesh['lat'=16,'lon'=16] {'lon'}, dimensions={0}, use_global_device_ids=true | all-gather | bytes 278528 | tf_op jit(solution)/shard_map/all_gather | solution.py:55
  369.6 2.8 stack.3
  372.4 10.8 %all-to-all-start = ((bf16[16,32,32,128]{3,2,1,0:T(8,128)(2,1)}), bf16[16,32,32,128]{3,2,1,0:T(8,128)(2,1)}, u32[]{:S(2)}, u32[]{:S(2)}) async-start(bf16[16,32,32,128]{3,2,1,0:T(8,128)(2,1)} %stack.3), calls=%async_computation | async-start | bytes 8388608 | tf_op jit(solution)/shard_map/all_to_all | solution.py:149
  386.1 4.5 compare_select_fusion.1
  390.6 5.4 %fusion.59 = s32[512]{0:T(512)S(1)} fusion(pred[512]{0:T(512)(128)(4,1)S(1)} %get-tuple-element.93, pred[512]{0:T(512)(128)(4,1)S(1)} %get-tuple-element.94, pred[512]{0:T(512)(128)(4,1)S(1)} %get-tuple-element.95, pred[512]{0:T(512)(128)(4,1)S(1)} %get-tuple-element.96, pred[512]{0:T(512)(128)(4,1)S(1)} %get-tuple-element.97, ...), kind=kLoop, calls=%fused_computation.145 | loop fusion | flops 8704 | bytes 8740 | tf_op jit(solution)/shard_map/add | solution.py:155
  396.8 43.6 %all-to-all-done = bf16[16,32,32,128]{3,2,1,0:T(8,128)(2,1)} async-done(((bf16[16,32,32,128]{3,2,1,0:T(8,128)(2,1)}), bf16[16,32,32,128]{3,2,1,0:T(8,128)(2,1)}, u32[]{:S(2)}, u32[]{:S(2)}) %all-to-all-start) | async-done | bytes 4194336 | tf_op jit(solution)/shard_map/all_to_all | solution.py:149
  440.4 3.3 copy.121
  443.7 1.6 fusion
  445.4 2.4 fusion.1
  447.8 4.4 divide_convert_fusion
  (110 shorter events, 21.0 us)
Async XLA Ops:
  0.0 396.1 %copy-start = (bf16[256,256]{1,0:T(8,128)(2,1)S(1)}, bf16[256,256]{1,0:T(8,128)(2,1)}, u32[]{:S(2)}) copy-start(bf16[256,256]{1,0:T(8,128)(2,1)} %param.25) | copy-start | bytes 393220
  2.0 5.8 %copy-start.8 = (s32[16,16]{1,0:T(8,128)S(1)}, s32[16,16]{1,0:T(8,128)}, u32[]{:S(2)}) copy-start(s32[16,16]{1,0:T(8,128)} %param.30) | copy-start | bytes 3076
  2.0 13.7 %copy-start.9 = (s32[512]{0:T(512)S(1)}, s32[512]{0:T(512)}, u32[]{:S(2)}) copy-start(s32[512]{0:T(512)} %param.31) | copy-start | bytes 6148
  3.4 149.1 %collective-permute-start.1 = (bf16[1,32,256]{2,1,0:T(8,128)(2,1)S(1)}, bf16[1,32,256]{2,1,0:T(8,128)(2,1)S(1)}, u32[]{:S(2)}, u32[]{:S(2)}) collective-permute-start(bf16[1,32,256]{2,1,0:T(8,128)(2,1)S(1)} %get-tuple-element.49), channel_id=1, source_target_pairs={{16,0},{32,16},{48,32},{64,48},{80,64},{96,80},{112,96},{128,112},... | collective-permute-start | bytes 49160 | tf_op jit(solution)/shard_map/ppermute | solution.py:19
  5.4 106.7 %collective-permute-start = (bf16[1,32,256]{2,1,0:T(8,128)(2,1)S(1)}, bf16[1,32,256]{2,1,0:T(8,128)(2,1)S(1)}, u32[]{:S(2)}, u32[]{:S(2)}) collective-permute-start(bf16[1,32,256]{2,1,0:T(8,128)(2,1)S(1)} %get-tuple-element.50), channel_id=1, source_target_pairs={{0,16},{16,32},{32,48},{48,64},{64,80},{80,96},{96,112},{112,128},... | collective-permute-start | bytes 49160 | tf_op jit(solution)/shard_map/ppermute | solution.py:19
  190.1 1.3 copy-start.3
  190.1 1.3 copy-start.10
  194.5 122.9 %collective-permute-start.3 = (bf16[1,32,256]{2,1,0:T(8,128)(2,1)S(1)}, bf16[1,32,256]{2,1,0:T(8,128)(2,1)S(1)}, u32[]{:S(2)}, u32[]{:S(2)}) collective-permute-start(bf16[1,32,256]{2,1,0:T(8,128)(2,1)S(1)} %get-tuple-element.43), channel_id=1, source_target_pairs={{16,0},{32,16},{48,32},{64,48},{80,64},{96,80},{112,96},{128,112},... | collective-permute-start | bytes 49160 | tf_op jit(solution)/shard_map/ppermute | solution.py:19
  196.4 80.7 %collective-permute-start.2 = (bf16[1,32,256]{2,1,0:T(8,128)(2,1)S(1)}, bf16[1,32,256]{2,1,0:T(8,128)(2,1)S(1)}, u32[]{:S(2)}, u32[]{:S(2)}) collective-permute-start(bf16[1,32,256]{2,1,0:T(8,128)(2,1)S(1)} %get-tuple-element.44), channel_id=1, source_target_pairs={{0,16},{16,32},{32,48},{48,64},{64,80},{80,96},{96,112},{112,128},... | collective-permute-start | bytes 49160 | tf_op jit(solution)/shard_map/ppermute | solution.py:19
  363.9 1.3 copy-start.4
  363.9 1.3 copy-start.11
  368.6 0.8 copy-start.6
  368.6 0.8 copy-start.7
  372.4 68.0 %all-to-all-start = ((bf16[16,32,32,128]{3,2,1,0:T(8,128)(2,1)}), bf16[16,32,32,128]{3,2,1,0:T(8,128)(2,1)}, u32[]{:S(2)}, u32[]{:S(2)}) async-start(bf16[16,32,32,128]{3,2,1,0:T(8,128)(2,1)} %stack.3), calls=%async_computation | async-start | bytes 8388608 | tf_op jit(solution)/shard_map/all_to_all | solution.py:149
  452.2 1.2 copy-start.5
  454.5 0.8 copy-start.2
  455.3 0.9 copy-start.1
